TPU v7x, 128 devices: a whole 4x4x4 slice. The times are simulated.
128 devices in a mesh: seq: 32 (over y, z, core), head: 4 (over x).
Axes of the slice: x: 4, y: 4, z: 4, core: 2. Of those that a mesh axis runs over, the one named last changes fastest.
Arguments:
- queries: bfloat16 [131072, 2048], P('seq', 'head'), may hold values from -6 to 6
- keys: bfloat16 [131072, 2048], P('seq', 'head'), may hold values from -0.59765625 to 0.59765625
- values: bfloat16 [131072, 2048], P('seq', 'head'), may hold values from -6 to 6
- norm_gain: float32 [2048], replicated, may hold values from 0.1 to 1.9
Outputs:
- normed: bfloat16 [131072, 2048], P(('seq', 'head'))
All inputs are finite; a program needn't handle non-finite values.
Results may differ from a plain program's by a relative error of at most 0.0058.
Values may be sent and summed in bfloat16 or wider, within the bound.
A program may use at most 128 MiB of HBM per device.

v0:
```python
import jax
import jax.numpy as jnp
from jax import lax
from jax.sharding import PartitionSpec as P

DH = 128
BLK = 512


def add_lower(piece, mine):
    ranks = jnp.arange(piece.shape[0], dtype=jnp.int32)
    keep = (ranks < mine).astype(jnp.float32)[:, None, None, None]
    return jnp.sum(piece * keep, axis=0)


def shards(queries, keys, values, norm_gain):
    rows, width = queries.shape
    heads = width // DH
    blocks = rows // BLK
    query_rows = queries.reshape(blocks, BLK, heads, DH)
    key_rows = keys.reshape(blocks, BLK, heads, DH)
    value_rows = values.reshape(blocks, BLK, heads, DH)
    block_state = jnp.einsum(
        "nbhd,nbhe->nhde", key_rows, value_rows, preferred_element_type=jnp.float32
    )
    total = jnp.sum(block_state, axis=0)
    mine = lax.axis_index("seq")
    before = add_lower(lax.all_gather(total[None], "seq", axis=0, tiled=True), mine)
    running = jnp.cumsum(block_state, axis=0)
    within = jnp.concatenate([jnp.zeros_like(block_state[:1]), running[:-1]], axis=0)
    prefix_low = (before[None] + within).astype(jnp.bfloat16)
    inter = jnp.einsum(
        "nbhd,nhde->nbhe", query_rows, prefix_low, preferred_element_type=jnp.float32
    )
    scores = jnp.einsum("nbhd,nchd->nhbc", query_rows, key_rows, preferred_element_type=jnp.float32)
    causal = jnp.arange(BLK)[:, None] >= jnp.arange(BLK)[None, :]
    scores = jnp.where(causal[None, None], scores, jnp.zeros_like(scores)).astype(jnp.bfloat16)
    intra = jnp.einsum("nhbc,nche->nbhe", scores, value_rows, preferred_element_type=jnp.float32)
    attention = (inter + intra).astype(jnp.bfloat16).reshape(rows, width)
    regrouped = lax.all_to_all(attention, "head", split_axis=0, concat_axis=1, tiled=True)
    widened = regrouped.astype(jnp.float32)
    meansq = jnp.mean(widened * widened, axis=-1, keepdims=True)
    return (widened * lax.rsqrt(meansq + 1e-06) * norm_gain[None, :]).astype(jnp.bfloat16)


def solution(mesh):
    return jax.shard_map(
        shards,
        mesh=mesh,
        in_specs=(P("seq", "head"), P("seq", "head"), P("seq", "head"), P()),
        out_specs=P(("seq", "head"), None),
        check_vma=False,
    )
```

profile of v0, /device:TPU:1, one launch (start us, length us, event | category | flops | bytes accessed | tf_op | source)
XLA Modules:
  0.0 208.3 jit_solution(7834512053648835471)
XLA Ops:
  6.5 0.0 all-gather.3.cloned.1.call-start
  6.5 6.9 %reshape.43 = bf16[8,512,4,128]{3,2,1,0:T(4,128)(2,1)} reshape(bf16[4096,512]{1,0:T(8,128)(2,1)} %param.5) | data formatting | bytes 8388608 | tf_op jit(solution)/shard_map/reshape | solution.py:21
  13.4 6.9 %reshape.44 = bf16[8,512,4,128]{3,2,1,0:T(4,128)(2,1)} reshape(bf16[4096,512]{1,0:T(8,128)(2,1)} %param.6) | data formatting | bytes 8388608 | tf_op jit(solution)/shard_map/reshape | solution.py:22
  20.4 5.9 %fusion.28 = (f32[4,128,128]{2,1,0:T(8,128)}, f32[8,4,128,128]{3,2,1,0:T(8,128)S(1)}) fusion(bf16[8,512,4,128]{3,2,1,0:T(4,128)(2,1)} %reshape.44, bf16[8,512,4,128]{3,2,1,0:T(4,128)(2,1)} %reshape.43), kind=kOutput, calls=%fused_computation.29 | convolution fusion | flops 537329664 | bytes 10747904 | tf_op jit(solution)/shard_map/nbhd,nbhe->nhde/dot_general | solution.py:23
  26.3 0.0 all-gather.3.cloned.1.call-update
  26.3 6.9 %reshape.45 = bf16[8,512,4,128]{3,2,1,0:T(4,128)(2,1)} reshape(bf16[4096,512]{1,0:T(8,128)(2,1)} %param.4) | data formatting | bytes 8388608 | tf_op jit(solution)/shard_map/reshape | solution.py:20
  33.2 1.9 fusion.29
  35.1 0.2 slice.4
  35.3 0.1 iota_compare_fusion
  35.4 47.7 %all-gather.3.cloned.1.call-done = f32[128,128,128]{2,1,0:T(8,128)} async-done(((f32[4,128,128]{2,1,0:T(8,128)}), f32[128,128,128]{2,1,0:T(8,128)}) %all-gather.3.cloned.1.call-update) | async-done | bytes 8388624 | tf_op jit(solution)/shard_map/all_gather | solution.py:28
  83.1 0.0 copy-start
  83.1 4.7 %multiply_reduce_fusion = f32[4,128,128]{2,1,0:T(8,128)S(1)} fusion(f32[32,4,128,128]{3,2,1,0:T(8,128)} %bitcast.16, f32[32]{0:T(128)S(1)} %compare_convert_fusion), kind=kLoop, calls=%fused_computation.13 | loop fusion | flops 4128768 | bytes 8650880 | tf_op jit(solution)/shard_map/reduce_sum | solution.py:13
  87.8 0.0 copy-done
  87.8 4.6 %fusion.15 = f32[8,4,128,512]{3,2,1,0:T(8,128)} fusion(bf16[8,512,4,128]{3,2,1,0:T(4,128)(2,1)S(1)} %copy-done, f32[7,4,128,128]{3,2,1,0:T(8,128)S(1)} %slice.4, f32[4,128,128]{2,1,0:T(8,128)S(1)} %multiply_reduce_fusion), kind=kOutput, calls=%fused_computation.18 | convolution fusion | flops 537919488 | bytes 14680064 | tf_op jit(solution)/shard_map/nbhd,nhde->nbhe/dot_general | solution.py:32
  92.4 16.4 %fusion.8 = bf16[8,512,4,128]{1,3,2,0:T(8,128)(2,1)} fusion(f32[8,4,128,512]{3,2,1,0:T(8,128)} %fusion.15, bf16[8,512,4,128]{3,2,1,0:T(4,128)(2,1)} %reshape.44, pred[512,512]{1,0:T(8,128)(4,1)S(1)} %iota_compare_fusion, bf16[8,512,4,128]{3,2,1,0:T(4,128)(2,1)} %reshape.43, bf16[8,512,4,128]{3,2,1,0:T(4,128)(2,1)} %reshape.45), kind=kOutput, calls=%fused_computation.12 | convolution fusion | flops 4315938816 | bytes 25427968 | tf_op jit(solution)/shard_map/nhbc,nche->nbhe/dot_general | solution.py:38
  108.9 7.4 %copy.37 = bf16[8,512,4,128]{3,2,1,0:T(4,128)(2,1)} copy(bf16[8,512,4,128]{1,3,2,0:T(8,128)(2,1)} %fusion.8) | data formatting | bytes 8388608 | tf_op jit(solution)/shard_map/convert_element_type | solution.py:39
  116.3 7.2 %all_to_all.10 = bf16[4,1024,512]{2,1,0:T(8,128)(2,1)} reshape(bf16[8,512,4,128]{3,2,1,0:T(4,128)(2,1)} %copy.37) | data formatting | bytes 8388608 | tf_op jit(solution)/shard_map/all_to_all | solution.py:40
  123.5 52.3 %all_to_all.13 = bf16[4,1024,512]{2,1,0:T(8,128)(2,1)S(1)} all-to-all(bf16[4,1024,512]{2,1,0:T(8,128)(2,1)} %all_to_all.10), channel_id=1, replica_groups=mesh['seq'=32,'head'=4] {'head'}, dimensions={0} | all-to-all | bytes 8388608 | tf_op jit(solution)/shard_map/all_to_all | solution.py:40
  175.8 0.9 fusion.5
  176.7 4.4 %convert_bitcast_fusion = f32[1024,4,512]{2,0,1:T(8,128)} fusion(bf16[4,1024,512]{2,1,0:T(8,128)(2,1)S(1)} %all_to_all.13), kind=kLoop, calls=%fused_computation.6 | loop fusion | flops 2097152 | bytes 12582912 | tf_op jit(solution)/shard_map/convert_element_type | solution.py:41
  181.1 0.0 copy-start.1
  181.1 8.7 %copy.38 = f32[1024,4,512]{0,2,1:T(8,128)} copy(f32[1024,4,512]{2,0,1:T(8,128)} %convert_bitcast_fusion) | data formatting | bytes 16777216 | tf_op jit(solution)/shard_map/convert_element_type | solution.py:41
  189.9 0.0 copy-done.1
  189.9 5.2 %fusion.7 = bf16[1024,2048]{0,1:T(8,128)(2,1)} fusion(f32[1024,4,512]{0,2,1:T(8,128)} %copy.38, f32[2048]{0:T(1024)S(1)} %copy-done.1, f32[1024]{0:T(1024)S(1)} %add_rsqrt_fusion), kind=kLoop, calls=%fused_computation.10 | loop fusion | flops 6291456 | bytes 12595200 | tf_op jit(solution)/shard_map/convert_element_type | solution.py:43
  195.1 6.4 %copy.39 = bf16[1024,2048]{1,0:T(8,128)(2,1)} copy(bf16[1024,2048]{0,1:T(8,128)(2,1)} %fusion.7) | data formatting | bytes 8388608 | tf_op jit(solution)/shard_map/convert_element_type | solution.py:43
  (2 shorter events, 0.0 us)
Async XLA Ops:
  6.5 76.6 %all-gather.3.cloned.1.call-start = ((), (), s32[]{:S(2)}) async-start(), calls=%async_computation.1 | async-start | bytes 8650752 | tf_op jit(solution)/shard_map/all_gather | solution.py:28
  83.1 4.7 %copy-start = (bf16[8,512,4,128]{3,2,1,0:T(4,128)(2,1)S(1)}, bf16[8,512,4,128]{3,2,1,0:T(4,128)(2,1)}, u32[]{:S(2)}) copy-start(bf16[8,512,4,128]{3,2,1,0:T(4,128)(2,1)} %reshape.45) | copy-start | bytes 12582916
  181.1 8.8 %copy-start.1 = (f32[2048]{0:T(1024)S(1)}, f32[2048]{0:T(1024)}, u32[]{:S(2)}) copy-start(f32[2048]{0:T(1024)} %param.7) | copy-start | bytes 24580
Sparse Core Ops, SparseCore 0:
  26.4 56.6 all-gather.2
where the time goes:
time: 210 us; the launch traced here: 208 us
  blocking collectives  52.3 us (25%)
  local copies, waits for them, and re-layouts  50.7 us (24%)
  waiting for transfers between devices  47.7 us (23%)
  matrix products  27 us (13%)
  other arithmetic  17.1 us (8%)
  between operations  13.5 us (6%)
    all_to_all x1, blocking collectives, shards(): lax.all_to_all(attention, 'head', split_axis=0, concat_axis=1, tiled=True)  52.3 us
    all_gather x1, waiting for transfers between devices, shards(): lax.all_gather(total[None], 'seq', axis=0, tiled=True)  47.7 us
    dot_general x1, matrix products, shards(): jnp.einsum('nhbc,nche->nbhe', scores, value_rows, preferred_element_type=...  16.4 us
    convert_element_type x1, local copies, waits for them, and re-layouts, shards(): widened = regrouped.astype(jnp.float32)  8.75 us
    convert_element_type x1, local copies, waits for them, and re-layouts, shards(): attention = (inter + intra).astype(jnp.bfloat16).reshape(rows, width)  7.44 us
    all_to_all x1, local copies, waits for them, and re-layouts, shards(): lax.all_to_all(attention, 'head', split_axis=0, concat_axis=1, tiled=True)  7.21 us
    reshape x1, local copies, waits for them, and re-layouts, shards(): value_rows = values.reshape(blocks, BLK, heads, DH)  6.93 us
    reshape x1, local copies, waits for them, and re-layouts, shards(): key_rows = keys.reshape(blocks, BLK, heads, DH)  6.91 us
  transfers between devices with their start and end apart: 1, of which 1 were waited for; matrix products, arithmetic and copies ran while one was open for 4% of the time, Pallas kernels for 0%

commit v1 on v0

--- a/solution.py
+++ b/solution.py
@@ -25,7 +25,12 @@
     )
     total = jnp.sum(block_state, axis=0)
     mine = lax.axis_index("seq")
-    before = add_lower(lax.all_gather(total[None], "seq", axis=0, tiled=True), mine)
+    before = add_lower(
+        jnp.concatenate(
+            lax.all_to_all(jnp.stack([total[None]] * lax.axis_size("seq")), "seq", 0, 0), axis=0
+        ),
+        mine,
+    )
     running = jnp.cumsum(block_state, axis=0)
     within = jnp.concatenate([jnp.zeros_like(block_state[:1]), running[:-1]], axis=0)
     prefix_low = (before[None] + within).astype(jnp.bfloat16)

time: 210 us -> 282 us (1.34)
  the two profiles are of different devices: /device:TPU:1 before, /device:TPU:32 now
where the time goes in v1:
time: 282 us; the launch traced here: 280 us
  waiting for transfers between devices  115 us (41%)
  local copies, waits for them, and re-layouts  57.1 us (20%)
  blocking collectives  52.9 us (19%)
  matrix products  27.6 us (10%)
  other arithmetic  19.2 us (7%)
  starting transfers between devices  8.26 us (3%)
    all_to_all x1, waiting for transfers between devices, shards(): lax.all_to_all(jnp.stack([total[None]] * lax.axis_size('seq')), 'seq', 0, 0)  115 us
    all_to_all x1, blocking collectives, shards(): lax.all_to_all(attention, 'head', split_axis=0, concat_axis=1, tiled=True)  52.9 us
    dot_general x1, matrix products, shards(): jnp.einsum('nhbc,nche->nbhe', scores, value_rows, preferred_element_type=...  16.4 us
    convert_element_type x1, local copies, waits for them, and re-layouts, shards(): widened = regrouped.astype(jnp.float32)  8.73 us
    all_to_all x1, starting transfers between devices, shards(): lax.all_to_all(jnp.stack([total[None]] * lax.axis_size('seq')), 'seq', 0, 0)  8.26 us
    convert_element_type x1, local copies, waits for them, and re-layouts, shards(): attention = (inter + intra).astype(jnp.bfloat16).reshape(rows, width)  7.44 us
    all_to_all x1, local copies, waits for them, and re-layouts, shards(): lax.all_to_all(attention, 'head', split_axis=0, concat_axis=1, tiled=True)  7.21 us
    reshape x1, local copies, waits for them, and re-layouts, shards(): query_rows = queries.reshape(blocks, BLK, heads, DH)  7.13 us
  transfers between devices with their start and end apart: 1, of which 1 were waited for; matrix products, arithmetic and copies ran while one was open for 3% of the time, Pallas kernels for 0%

profile of v1, /device:TPU:32, one launch (start us, length us, event | category | flops | bytes accessed | tf_op | source)
XLA Modules:
  0.0 280.3 jit_solution(17400943609982083812)
XLA Ops:
  0.0 6.9 %reshape.48 = bf16[8,512,4,128]{3,2,1,0:T(4,128)(2,1)} reshape(bf16[4096,512]{1,0:T(8,128)(2,1)} %param.5) | data formatting | bytes 8388608 | tf_op jit(solution)/shard_map/reshape | solution.py:21
  6.9 6.9 %reshape.49 = bf16[8,512,4,128]{3,2,1,0:T(4,128)(2,1)} reshape(bf16[4096,512]{1,0:T(8,128)(2,1)} %param.6) | data formatting | bytes 8388608 | tf_op jit(solution)/shard_map/reshape | solution.py:22
  13.9 6.5 %fusion.29 = (f32[4,128,128]{2,1,0:T(8,128)S(1)}, f32[8,4,128,128]{3,2,1,0:T(8,128)}) fusion(bf16[8,512,4,128]{3,2,1,0:T(4,128)(2,1)} %reshape.49, bf16[8,512,4,128]{3,2,1,0:T(4,128)(2,1)} %reshape.48), kind=kOutput, calls=%fused_computation.30 | convolution fusion | flops 537329664 | bytes 10747904 | tf_op jit(solution)/shard_map/nbhd,nbhe->nhde/dot_general | solution.py:23
  20.4 4.3 %stack.3 = f32[32,1,4,128,128]{4,3,2,1,0:T(8,128)} broadcast(f32[4,128,128]{2,1,0:T(8,128)S(1)} %get-tuple-element.5), dimensions={2,3,4} | broadcast | bytes 8650752 | tf_op jit(solution)/shard_map/stack | solution.py:30
  24.6 8.3 %all-to-all-start = ((f32[32,1,4,128,128]{4,3,2,1,0:T(8,128)}), f32[32,1,4,128,128]{4,3,2,1,0:T(8,128)}, u32[]{:S(2)}, u32[]{:S(2)}) async-start(f32[32,1,4,128,128]{4,3,2,1,0:T(8,128)} %stack.3), calls=%async_computation | async-start | bytes 16777216 | tf_op jit(solution)/shard_map/all_to_all | solution.py:30
  32.9 1.8 fusion.30
  34.7 0.0 copy-start.2
  34.7 7.1 %reshape.51 = bf16[8,512,4,128]{3,2,1,0:T(4,128)(2,1)} reshape(bf16[4096,512]{1,0:T(8,128)(2,1)} %param.4) | data formatting | bytes 8388608 | tf_op jit(solution)/shard_map/reshape | solution.py:20
  41.8 0.0 copy-done.2
  41.8 0.1 iota_compare_fusion
  41.9 0.0 slice-start
  41.9 115.2 %all-to-all-done = f32[32,1,4,128,128]{4,3,2,1,0:T(8,128)} async-done(((f32[32,1,4,128,128]{4,3,2,1,0:T(8,128)}), f32[32,1,4,128,128]{4,3,2,1,0:T(8,128)}, u32[]{:S(2)}, u32[]{:S(2)}) %all-to-all-start) | async-done | bytes 8388640 | tf_op jit(solution)/shard_map/all_to_all | solution.py:30
  157.2 0.0 copy-start.1
  157.2 4.7 %fusion.9 = f32[4,128,128]{2,1,0:T(8,128)S(1)} fusion(f32[32,1,4,128,128]{4,3,2,1,0:T(8,128)} %all-to-all-done, f32[32]{0:T(128)S(1)} %compare_convert_fusion), kind=kLoop, calls=%fused_computation.14 | loop fusion | flops 4128768 | bytes 8650880 | tf_op jit(solution)/shard_map/reduce_sum | solution.py:13
  161.8 0.0 slice-done
  161.8 0.0 copy-done.1
  161.8 4.6 %fusion.16 = f32[8,4,128,512]{3,2,1,0:T(8,128)} fusion(bf16[8,512,4,128]{3,2,1,0:T(4,128)(2,1)S(1)} %copy-done.1, f32[7,4,128,128]{3,2,1,0:T(8,128)S(1)} %slice-done, f32[4,128,128]{2,1,0:T(8,128)S(1)} %fusion.9), kind=kOutput, calls=%fused_computation.19 | convolution fusion | flops 537919488 | bytes 14680064 | tf_op jit(solution)/shard_map/nbhd,nhde->nbhe/dot_general | solution.py:37
  166.5 16.4 %fusion.8 = bf16[8,512,4,128]{1,3,2,0:T(8,128)(2,1)} fusion(f32[8,4,128,512]{3,2,1,0:T(8,128)} %fusion.16, bf16[8,512,4,128]{3,2,1,0:T(4,128)(2,1)} %reshape.49, pred[512,512]{1,0:T(8,128)(4,1)S(1)} %iota_compare_fusion, bf16[8,512,4,128]{3,2,1,0:T(4,128)(2,1)} %reshape.48, bf16[8,512,4,128]{3,2,1,0:T(4,128)(2,1)} %reshape.51), kind=kOutput, calls=%fused_computation.12 | convolution fusion | flops 4315938816 | bytes 25427968 | tf_op jit(solution)/shard_map/nhbc,nche->nbhe/dot_general | solution.py:43
  182.9 7.4 %copy.48 = bf16[8,512,4,128]{3,2,1,0:T(4,128)(2,1)} copy(bf16[8,512,4,128]{1,3,2,0:T(8,128)(2,1)} %fusion.8) | data formatting | bytes 8388608 | tf_op jit(solution)/shard_map/convert_element_type | solution.py:44
  190.3 7.2 %all_to_all.14 = bf16[4,1024,512]{2,1,0:T(8,128)(2,1)} reshape(bf16[8,512,4,128]{3,2,1,0:T(4,128)(2,1)} %copy.48) | data formatting | bytes 8388608 | tf_op jit(solution)/shard_map/all_to_all | solution.py:45
  197.5 52.9 %all_to_all.18 = bf16[4,1024,512]{2,1,0:T(8,128)(2,1)S(1)} all-to-all(bf16[4,1024,512]{2,1,0:T(8,128)(2,1)} %all_to_all.14), channel_id=1, replica_groups=mesh['seq'=32,'head'=4] {'head'}, dimensions={0} | all-to-all | bytes 8388608 | tf_op jit(solution)/shard_map/all_to_all | solution.py:45
  250.4 0.0 copy-start
  250.4 2.0 copy-done
  252.4 4.4 %convert_bitcast_fusion = f32[1024,4,512]{2,0,1:T(8,128)} fusion(bf16[4,1024,512]{2,1,0:T(8,128)(2,1)S(1)} %all_to_all.18), kind=kLoop, calls=%fused_computation.6 | loop fusion | flops 2097152 | bytes 12582912 | tf_op jit(solution)/shard_map/convert_element_type | solution.py:46
  256.8 8.7 %copy.49 = f32[1024,4,512]{0,2,1:T(8,128)} copy(f32[1024,4,512]{2,0,1:T(8,128)} %convert_bitcast_fusion) | data formatting | bytes 16777216 | tf_op jit(solution)/shard_map/convert_element_type | solution.py:46
  265.6 0.0 copy-start.3
  265.6 3.1 %fusion.5 = f32[1024]{0:T(1024)S(1)} fusion(bf16[4,1024,512]{2,1,0:T(8,128)(2,1)} %copy-done), kind=kLoop, calls=%fused_computation.7 | loop fusion | flops 6290432 | bytes 4198400 | tf_op jit(solution)/shard_map/reduce_sum | solution.py:47
  268.7 0.0 copy-done.3
  268.7 5.2 %fusion.7 = bf16[1024,2048]{0,1:T(8,128)(2,1)} fusion(f32[1024,4,512]{0,2,1:T(8,128)} %copy.49, f32[2048]{0:T(1024)S(1)} %copy-done.3, f32[1024]{0:T(1024)S(1)} %add_rsqrt_fusion), kind=kLoop, calls=%fused_computation.10 | loop fusion | flops 6291456 | bytes 12595200 | tf_op jit(solution)/shard_map/convert_element_type | solution.py:48
  273.9 6.4 %copy.50 = bf16[1024,2048]{1,0:T(8,128)(2,1)} copy(bf16[1024,2048]{0,1:T(8,128)(2,1)} %fusion.7) | data formatting | bytes 8388608 | tf_op jit(solution)/shard_map/convert_element_type | solution.py:48
  (2 shorter events, 0.0 us)
Async XLA Ops:
  24.6 132.5 %all-to-all-start = ((f32[32,1,4,128,128]{4,3,2,1,0:T(8,128)}), f32[32,1,4,128,128]{4,3,2,1,0:T(8,128)}, u32[]{:S(2)}, u32[]{:S(2)}) async-start(f32[32,1,4,128,128]{4,3,2,1,0:T(8,128)} %stack.3), calls=%async_computation | async-start | bytes 16777216 | tf_op jit(solution)/shard_map/all_to_all | solution.py:30
  34.7 7.1 %copy-start.2 = (f32[8,4,128,128]{3,2,1,0:T(8,128)}, f32[8,4,128,128]{3,2,1,0:T(8,128)S(1)}, u32[]{:S(2)}) copy-start(f32[8,4,128,128]{3,2,1,0:T(8,128)S(1)} %fusion.30) | copy-start | bytes 6291460
  41.9 119.9 %slice-start = ((f32[8,4,128,128]{3,2,1,0:T(8,128)}), f32[7,4,128,128]{3,2,1,0:T(8,128)S(1)}, s32[]{:S(2)}) async-start(f32[8,4,128,128]{3,2,1,0:T(8,128)} %copy-done.2), calls=%async_computation.2 | async-start | bytes 3670016 | tf_op jit(solution)/shard_map/slice | solution.py:35
  157.2 4.7 %copy-start.1 = (bf16[8,512,4,128]{3,2,1,0:T(4,128)(2,1)S(1)}, bf16[8,512,4,128]{3,2,1,0:T(4,128)(2,1)}, u32[]{:S(2)}) copy-start(bf16[8,512,4,128]{3,2,1,0:T(4,128)(2,1)} %reshape.51) | copy-start | bytes 12582916
  250.4 2.0 copy-start
  265.6 3.1 %copy-start.3 = (f32[2048]{0:T(1024)S(1)}, f32[2048]{0:T(1024)}, u32[]{:S(2)}) copy-start(f32[2048]{0:T(1024)} %param.7) | copy-start | bytes 24580
